TPU v7x, 32 devices: a whole 2x2x4 slice. The times are simulated.
32 devices in a mesh: rep: 8 (over z, x), shard: 4 (over y, core).
Axes of the slice: x: 2, y: 2, z: 4, core: 2. Of those that a mesh axis runs over, the one named last changes fastest.
Arguments:
- hidden_in: bfloat16 [8, 512, 960], P('rep', 'shard'), may hold values from -6 to 6
- out_grad: bfloat16 [8, 512, 960], P('rep', 'shard'), may hold values from -6 to 6
- norm1_gain: bfloat16 [960], P('shard'), may hold values from 0.5 to 1.5
- q_weight: bfloat16 [960, 960], P('shard'), may hold values from -0.1875 to 0.1875
- k_weight: bfloat16 [960, 320], P('shard'), may hold values from -0.1875 to 0.1875
- v_weight: bfloat16 [960, 320], P('shard'), may hold values from -0.1875 to 0.1875
- o_weight: bfloat16 [960, 960], P(None, 'shard'), may hold values from -1.5 to 1.5
- norm2_gain: bfloat16 [960], P('shard'), may hold values from 0.5 to 1.5
- gate_weight: bfloat16 [960, 2560], P('shard'), may hold values from -0.1875 to 0.1875
- up_weight: bfloat16 [960, 2560], P('shard'), may hold values from -0.1875 to 0.1875
- down_weight: bfloat16 [2560, 960], P('shard'), may hold values from -0.125 to 0.125
Outputs:
- output: float32 [8, 512, 960], P('rep', 'shard')
- input_grad: float32 [8, 512, 960], P('rep', 'shard')
- norm1_gain_grad: float32 [960], P('shard')
- q_weight_grad: float32 [960, 960], P('shard')
- k_weight_grad: float32 [960, 320], P('shard')
- v_weight_grad: float32 [960, 320], P('shard')
- o_weight_grad: float32 [960, 960], P(None, 'shard')
- norm2_gain_grad: float32 [960], P('shard')
- gate_weight_grad: float32 [960, 2560], P('shard')
- up_weight_grad: float32 [960, 2560], P('shard')
- down_weight_grad: float32 [2560, 960], P('shard')
All inputs are finite; a program needn't handle non-finite values.
Results may differ from a plain program's by a relative error of at most 0.02.
Values may be sent and summed in bfloat16 or wider, within the bound.
No kernel may reach another device: no remote copies, remote signals or barrier semaphores. Data moves between devices by JAX's collectives and lax.ppermute only.
A program may use at most 192 MiB of HBM per device.

v0:
```python
from functools import partial
import jax
import jax.numpy as jnp
from jax import lax
from jax.sharding import PartitionSpec as P

HQ = 15
KEY_VALUE_HEADS = 5
HEAD_SIZE = 64
QD = 960
KVD = 320
QUERY_PER_KV = 3
EPSILON = 1e-05
SCALE = 0.125
NEGATIVE = -1e30
THETA = 10000.0


def rms_inverse(rows):
    return lax.rsqrt(jnp.mean(rows * rows, axis=-1, keepdims=True) + EPSILON)


def rope_tables(positions):
    half = HEAD_SIZE // 2
    freqs = THETA ** (-(jnp.arange(half, dtype=jnp.float32) * 2.0 / HEAD_SIZE))
    angles = positions.astype(jnp.float32)[:, None] * freqs[None, :]
    return (jnp.cos(angles)[:, None, :], jnp.sin(angles)[:, None, :])


def rotate(tensor, cosine_table, sine_table):
    half = HEAD_SIZE // 2
    first, second = (tensor[..., :half], tensor[..., half:])
    return jnp.concatenate(
        [first * cosine_table - second * sine_table, second * cosine_table + first * sine_table],
        axis=-1,
    )


def inverse_rotary(tensor, cosine_table, sine_table):
    half = HEAD_SIZE // 2
    first, second = (tensor[..., :half], tensor[..., half:])
    return jnp.concatenate(
        [first * cosine_table + second * sine_table, second * cosine_table - first * sine_table],
        axis=-1,
    )


def head_scores(query_rows, keys, query_pos, key_pos):
    scores = jnp.einsum("ngd,ld->gnl", query_rows, keys, preferred_element_type=jnp.float32) * SCALE
    allowed = key_pos[None, None, :] <= query_pos[None, :, None]
    return (jnp.where(allowed, scores, NEGATIVE), allowed)


def head_forward(inputs, query_pos, key_pos):
    query_rows, keys, value_rows = inputs
    scores, allowed = head_scores(query_rows, keys, query_pos, key_pos)
    log_total = jax.nn.logsumexp(scores, axis=-1)
    probs = jnp.where(allowed, jnp.exp(scores - log_total[..., None]), 0.0)
    attended_rows = jnp.einsum(
        "gnl,ld->ngd", probs.astype(jnp.bfloat16), value_rows, preferred_element_type=jnp.float32
    )
    return (attended_rows, log_total)


def head_backward(inputs, query_pos, key_pos):
    query_rows, keys, value_rows, log_total, attention_gradient, attended_rows = inputs
    scores, allowed = head_scores(query_rows, keys, query_pos, key_pos)
    probs = jnp.where(allowed, jnp.exp(scores - log_total[..., None]), 0.0)
    probs_b = probs.astype(jnp.bfloat16)
    value_grad = jnp.einsum(
        "gnl,ngd->ld", probs_b, attention_gradient, preferred_element_type=jnp.float32
    )
    grad_prob = jnp.einsum(
        "ngd,ld->gnl", attention_gradient, value_rows, preferred_element_type=jnp.float32
    )
    delta = jnp.transpose(
        jnp.sum(attention_gradient.astype(jnp.float32) * attended_rows.astype(jnp.float32), axis=-1)
    )
    grad_score = (probs * (grad_prob - delta[..., None]) * SCALE).astype(jnp.bfloat16)
    query_grad = jnp.einsum("gnl,ld->ngd", grad_score, keys, preferred_element_type=jnp.float32)
    key_grad = jnp.einsum("gnl,ngd->ld", grad_score, query_rows, preferred_element_type=jnp.float32)
    return (query_grad, key_grad, value_grad)


def outer(left, right):
    return lax.dot_general(
        left, right, (((0,), (0,)), ((), ())), preferred_element_type=jnp.float32
    )


def back(left, weight):
    return lax.dot_general(
        left, weight, (((1,), (1,)), ((), ())), preferred_element_type=jnp.float32
    )


def local(
    hidden_in,
    out_grad,
    norm1_gain,
    q_weight,
    k_weight,
    v_weight,
    o_weight,
    norm2_gain,
    gate_weight,
    up_weight,
    down_weight,
):
    params = (
        lax.all_gather(norm1_gain, "shard", axis=0, tiled=True),
        lax.all_gather(q_weight, "shard", axis=0, tiled=True),
        lax.all_gather(k_weight, "shard", axis=0, tiled=True),
        lax.all_gather(v_weight, "shard", axis=0, tiled=True),
        lax.all_gather(o_weight, "shard", axis=1, tiled=True),
        lax.all_gather(norm2_gain, "shard", axis=0, tiled=True),
        lax.all_gather(gate_weight, "shard", axis=0, tiled=True),
        lax.all_gather(up_weight, "shard", axis=0, tiled=True),
        lax.all_gather(down_weight, "shard", axis=0, tiled=True),
    )
    gain_one, w_query, key_matrix, value_matrix, w_out, gain_two, w_gate, w_up, w_down = params
    token_count = hidden_in.shape[1]
    sequence_length_total = token_count * lax.axis_size("shard")
    query_pos = lax.axis_index("shard") * token_count + jnp.arange(token_count, dtype=jnp.int32)
    key_pos = jnp.arange(sequence_length_total, dtype=jnp.int32)
    x_full = hidden_in[0].astype(jnp.float32)
    inv_one = rms_inverse(x_full)
    normed_one = x_full * inv_one
    gain_one_f = gain_one.astype(jnp.float32)
    first_input = (normed_one * gain_one_f).astype(jnp.bfloat16)
    cosine_table, sine_table = rope_tables(query_pos)
    query_raw = jnp.dot(first_input, w_query, preferred_element_type=jnp.float32).reshape(
        token_count, HQ, HEAD_SIZE
    )
    query_rows = rotate(query_raw, cosine_table, sine_table).astype(jnp.bfloat16)
    unrotated_key = jnp.dot(first_input, key_matrix, preferred_element_type=jnp.float32).reshape(
        token_count, KEY_VALUE_HEADS, HEAD_SIZE
    )
    keys_own = (
        rotate(unrotated_key, cosine_table, sine_table)
        .astype(jnp.bfloat16)
        .reshape(token_count, KVD)
    )
    values_own = jnp.dot(first_input, value_matrix, preferred_element_type=jnp.float32).astype(
        jnp.bfloat16
    )
    gathered_keys, gathered_values = (
        lax.all_gather(keys_own, "shard", axis=0, tiled=True),
        lax.all_gather(values_own, "shard", axis=0, tiled=True),
    )
    query_head_rows = jnp.transpose(
        query_rows.reshape(token_count, KEY_VALUE_HEADS, QUERY_PER_KV, HEAD_SIZE), (1, 0, 2, 3)
    )
    key_head_rows = jnp.transpose(
        gathered_keys.reshape(sequence_length_total, KEY_VALUE_HEADS, HEAD_SIZE), (1, 0, 2)
    )
    value_head_rows = jnp.transpose(
        gathered_values.reshape(sequence_length_total, KEY_VALUE_HEADS, HEAD_SIZE), (1, 0, 2)
    )
    att_heads, log_total = lax.map(
        partial(head_forward, query_pos=query_pos, key_pos=key_pos),
        (query_head_rows, key_head_rows, value_head_rows),
    )
    attended_rows = (
        jnp.transpose(att_heads, (1, 0, 2, 3)).reshape(token_count, QD).astype(jnp.bfloat16)
    )
    x_one = x_full + jnp.dot(attended_rows, w_out, preferred_element_type=jnp.float32)
    inv_two = rms_inverse(x_one)
    normed_two = x_one * inv_two
    gain_two_f = gain_two.astype(jnp.float32)
    input_two = (normed_two * gain_two_f).astype(jnp.bfloat16)
    gate = jnp.dot(input_two, w_gate, preferred_element_type=jnp.float32)
    upward = jnp.dot(input_two, w_up, preferred_element_type=jnp.float32)
    sigma = jax.nn.sigmoid(gate)
    silu_gate = gate * sigma
    hidden_act = (silu_gate * upward).astype(jnp.bfloat16)
    output = x_one + jnp.dot(hidden_act, w_down, preferred_element_type=jnp.float32)
    params = (
        lax.all_gather(norm1_gain, "shard", axis=0, tiled=True),
        lax.all_gather(q_weight, "shard", axis=0, tiled=True),
        lax.all_gather(k_weight, "shard", axis=0, tiled=True),
        lax.all_gather(v_weight, "shard", axis=0, tiled=True),
        lax.all_gather(o_weight, "shard", axis=1, tiled=True),
        lax.all_gather(norm2_gain, "shard", axis=0, tiled=True),
        lax.all_gather(gate_weight, "shard", axis=0, tiled=True),
        lax.all_gather(up_weight, "shard", axis=0, tiled=True),
        lax.all_gather(down_weight, "shard", axis=0, tiled=True),
    )
    gain_one, w_query, key_matrix, value_matrix, w_out, gain_two, w_gate, w_up, w_down = params
    gain_one_f = gain_one.astype(jnp.float32)
    gain_two_f = gain_two.astype(jnp.float32)
    cotangent = out_grad[0]
    grad_hidden = back(cotangent, w_down)
    grad_gate = (grad_hidden * upward * sigma * (1.0 + gate * (1.0 - sigma))).astype(jnp.bfloat16)
    grad_upward = (grad_hidden * silu_gate).astype(jnp.bfloat16)
    grad_in_two = back(grad_gate, w_gate) + back(grad_upward, w_up)
    grad_gain_two = jnp.sum(grad_in_two * normed_two, axis=0)
    grad_norm_two = grad_in_two * gain_two_f
    grad_x_one = cotangent.astype(jnp.float32) + inv_two * (
        grad_norm_two - normed_two * jnp.mean(grad_norm_two * normed_two, axis=-1, keepdims=True)
    )
    grad_x_one_b = grad_x_one.astype(jnp.bfloat16)
    attention_gradient = back(grad_x_one_b, w_out).astype(jnp.bfloat16)
    attention_head_gradient = jnp.transpose(
        attention_gradient.reshape(token_count, KEY_VALUE_HEADS, QUERY_PER_KV, HEAD_SIZE),
        (1, 0, 2, 3),
    )
    attention_heads_bf16 = jnp.transpose(
        attended_rows.reshape(token_count, KEY_VALUE_HEADS, QUERY_PER_KV, HEAD_SIZE), (1, 0, 2, 3)
    )
    q_grad, k_grad, v_grad = lax.map(
        partial(head_backward, query_pos=query_pos, key_pos=key_pos),
        (
            query_head_rows,
            key_head_rows,
            value_head_rows,
            log_total,
            attention_head_gradient,
            attention_heads_bf16,
        ),
    )
    key_grad_all = jnp.transpose(k_grad, (1, 0, 2)).reshape(sequence_length_total, KVD)
    value_grad_all = jnp.transpose(v_grad, (1, 0, 2)).reshape(sequence_length_total, KVD)
    local_key_gradient, value_grad_own = (
        lax.psum_scatter(
            key_grad_all.astype(jnp.bfloat16), "shard", scatter_dimension=0, tiled=True
        ).astype(jnp.float32),
        lax.psum_scatter(
            value_grad_all.astype(jnp.bfloat16), "shard", scatter_dimension=0, tiled=True
        ).astype(jnp.float32),
    )
    query_grad = jnp.transpose(q_grad, (1, 0, 2, 3)).reshape(token_count, HQ, HEAD_SIZE)
    grad_q = (
        inverse_rotary(query_grad, cosine_table, sine_table)
        .reshape(token_count, QD)
        .astype(jnp.bfloat16)
    )
    grad_k = (
        inverse_rotary(
            local_key_gradient.reshape(token_count, KEY_VALUE_HEADS, HEAD_SIZE),
            cosine_table,
            sine_table,
        )
        .reshape(token_count, KVD)
        .astype(jnp.bfloat16)
    )
    grad_v = value_grad_own.astype(jnp.bfloat16)
    grad_in_one = back(grad_q, w_query) + back(grad_k, key_matrix) + back(grad_v, value_matrix)
    grad_gain_one = jnp.sum(grad_in_one * normed_one, axis=0)
    grad_norm_one = grad_in_one * gain_one_f
    grad_input = grad_x_one + inv_one * (
        grad_norm_one - normed_one * jnp.mean(grad_norm_one * normed_one, axis=-1, keepdims=True)
    )
    grad_down = outer(hidden_act, cotangent)
    grad_wgate = outer(input_two, grad_gate)
    grad_wup = outer(input_two, grad_upward)
    grad_wout = outer(attended_rows, grad_x_one_b)
    grad_wquery = outer(first_input, grad_q)
    grad_wkey = outer(first_input, grad_k)
    grad_wvalue = outer(first_input, grad_v)
    owned = (
        lax.psum_scatter(
            grad_gain_one.astype(jnp.bfloat16), "shard", scatter_dimension=0, tiled=True
        ).astype(jnp.float32),
        lax.psum_scatter(
            grad_wquery.astype(jnp.bfloat16), "shard", scatter_dimension=0, tiled=True
        ).astype(jnp.float32),
        lax.psum_scatter(
            grad_wkey.astype(jnp.bfloat16), "shard", scatter_dimension=0, tiled=True
        ).astype(jnp.float32),
        lax.psum_scatter(
            grad_wvalue.astype(jnp.bfloat16), "shard", scatter_dimension=0, tiled=True
        ).astype(jnp.float32),
        lax.psum_scatter(
            grad_wout.astype(jnp.bfloat16), "shard", scatter_dimension=1, tiled=True
        ).astype(jnp.float32),
        lax.psum_scatter(
            grad_gain_two.astype(jnp.bfloat16), "shard", scatter_dimension=0, tiled=True
        ).astype(jnp.float32),
        lax.psum_scatter(
            grad_wgate.astype(jnp.bfloat16), "shard", scatter_dimension=0, tiled=True
        ).astype(jnp.float32),
        lax.psum_scatter(
            grad_wup.astype(jnp.bfloat16), "shard", scatter_dimension=0, tiled=True
        ).astype(jnp.float32),
        lax.psum_scatter(
            grad_down.astype(jnp.bfloat16), "shard", scatter_dimension=0, tiled=True
        ).astype(jnp.float32),
    )
    matrices = (owned[1], owned[2], owned[3], owned[4], owned[6], owned[7], owned[8])
    flat_all = jnp.concatenate([matrix.reshape(-1) for matrix in matrices], axis=0)
    share = lax.psum_scatter(
        flat_all.astype(jnp.bfloat16), "rep", scatter_dimension=0, tiled=True
    ).astype(jnp.float32)
    whole = lax.all_gather(share.astype(jnp.bfloat16), "rep", axis=0, tiled=True).astype(
        share.dtype
    )
    gains_sum = lax.psum((owned[0], owned[5]), "rep")
    pieces_back = []
    offset = 0
    for matrix in matrices:
        length = matrix.size
        pieces_back.append(whole[offset : offset + length].reshape(matrix.shape))
        offset = offset + length
    return (
        output[None],
        grad_input[None],
        gains_sum[0],
        pieces_back[0],
        pieces_back[1],
        pieces_back[2],
        pieces_back[3],
        gains_sum[1],
        pieces_back[4],
        pieces_back[5],
        pieces_back[6],
    )


def solution(mesh):
    placed = (
        P("rep", "shard", None),
        P("rep", "shard", None),
        P("shard"),
        P("shard", None),
        P("shard", None),
        P("shard", None),
        P(None, "shard"),
        P("shard"),
        P("shard", None),
        P("shard", None),
        P("shard", None),
    )
    return jax.shard_map(
        local,
        mesh=mesh,
        in_specs=placed,
        out_specs=(
            P("rep", "shard", None),
            P("rep", "shard", None),
            P("shard"),
            P("shard", None),
            P("shard", None),
            P("shard", None),
            P(None, "shard"),
            P("shard"),
            P("shard", None),
            P("shard", None),
            P("shard", None),
        ),
        check_vma=False,
    )
```

profile of v0, /device:TPU:0, one launch (start us, length us, event | category | flops | bytes accessed | tf_op | source)
XLA Modules:
  0.0 838.1 jit_solution(9748543989205862080)
XLA Ops:
  13.9 8.4 all-reduce.7
  22.5 11.5 %all-gather.1 = bf16[4,240,320]{1,2,0:T(8,128)(2,1)S(1)} all-gather(bf16[1,240,320]{1,2,0:T(8,128)(2,1)S(1)} %bitcast.327), channel_id=1, replica_groups=mesh['rep'=8,'shard'=4] {'shard'}, dimensions={0}, use_global_device_ids=true | all-gather | bytes 768000 | tf_op jit(solution)/shard_map/all_gather | solution.py:113
  35.7 6.3 all_gather.49
  42.0 8.0 all-gather
  51.5 8.6 %all_gather.47 = bf16[512,320]{0,1:T(8,128)(2,1)S(1)} all-gather(bf16[128,320]{0,1:T(8,128)(2,1)S(1)} %convolution_convert_fusion.8), channel_id=1, replica_groups=mesh['rep'=8,'shard'=4] {'shard'}, dimensions={0}, use_global_device_ids=true | all-gather | bytes 409600 | tf_op jit(solution)/shard_map/all_gather | solution.py:149
  71.3 32.4 %all-gather.13.cloned.1.call-done = bf16[960,2560]{1,0:T(8,128)(2,1)} async-done(((bf16[240,2560]{1,0:T(8,128)(2,1)}), bf16[960,2560]{1,0:T(8,128)(2,1)}) %all-gather.13.cloned.1.call-update) | async-done | bytes 4915216 | tf_op jit(solution)/shard_map/all_gather | solution.py:117
  108.0 35.7 %all-gather.15.cloned.1.call-done = bf16[960,2560]{1,0:T(8,128)(2,1)} async-done(((bf16[240,2560]{1,0:T(8,128)(2,1)}), bf16[960,2560]{1,0:T(8,128)(2,1)}) %all-gather.15.cloned.1.call-update) | async-done | bytes 4915216 | tf_op jit(solution)/shard_map/all_gather | solution.py:118
  148.0 35.6 %all-gather.17.cloned.1.call-done = bf16[2560,960]{0,1:T(8,128)(2,1)} async-done(((bf16[640,960]{0,1:T(8,128)(2,1)}), bf16[2560,960]{0,1:T(8,128)(2,1)}) %all-gather.17.cloned.1.call-update) | async-done | bytes 4915216 | tf_op jit(solution)/shard_map/all_gather | solution.py:119
  183.6 5.3 multiply_convert_fusion
  196.7 26.1 %while.31 = (s32[]{:T(128)}, f32[5,128,3,64]{1,3,2,0:T(8,128)S(1)}, bf16[5,512,64]{1,2,0:T(8,128)(2,1)}, bf16[5,512,64]{1,2,0:T(8,128)(2,1)}, bf16[5,512,64]{1,2...) while((s32[]{:T(128)}, f32[5,128,3,64]{1,3,2,0:T(8,128)S(1)}, ...), condition=%wide.region_9.10_spmd.clone.clone, body=%wide.region_7.9_spmd.clone.sunk.clone | while | flops 127762176 | bytes 4536441 | solution.py:211
  226.9 18.9 %reduce-scatter.28.cloned.1.call-done = bf16[128,320]{1,0:T(8,128)(2,1)} async-done(((bf16[512,320]{1,0:T(8,128)(2,1)}), bf16[128,320]{1,0:T(8,128)(2,1)}) %reduce-scatter.28.cloned.1.call-update) | async-done | bytes 81936
  248.6 21.1 %reduce-scatter.30.cloned.1.call-done = bf16[128,320]{1,0:T(8,128)(2,1)} async-done(((bf16[512,320]{1,0:T(8,128)(2,1)}), bf16[128,320]{1,0:T(8,128)(2,1)}) %reduce-scatter.30.cloned.1.call-update) | async-done | bytes 81936
  293.2 7.9 copy.68
  302.3 19.6 %reduce-scatter.34.cloned.1.call-done = bf16[240,320]{1,0:T(8,128)(2,1)} async-done(((bf16[960,320]{1,0:T(8,128)(2,1)}), bf16[240,320]{1,0:T(8,128)(2,1)}) %reduce-scatter.34.cloned.1.call-update) | async-done | bytes 153616 | tf_op jit(solution)/shard_map/reduce_scatter | solution.py:271
  323.1 32.2 %reduce-scatter.22.cloned.1.call-done = bf16[240,960]{1,0:T(8,128)(2,1)} async-done(((bf16[960,960]{1,0:T(8,128)(2,1)}), bf16[240,960]{1,0:T(8,128)(2,1)}) %reduce-scatter.22.cloned.1.call-update) | async-done | bytes 460816 | tf_op jit(solution)/shard_map/reduce_scatter | solution.py:265
  357.7 31.1 %reduce-scatter.36.cloned.1.call-done = bf16[240,960]{1,0:T(8,128)(2,1)} async-done(((bf16[960,960]{1,0:T(8,128)(2,1)}), bf16[240,960]{1,0:T(8,128)(2,1)}) %reduce-scatter.36.cloned.1.call-update) | async-done | bytes 460816
  393.3 47.2 %reduce-scatter.24.cloned.1.call-done = bf16[240,2560]{1,0:T(8,128)(2,1)} async-done(((bf16[960,2560]{1,0:T(8,128)(2,1)}), bf16[240,2560]{1,0:T(8,128)(2,1)}) %reduce-scatter.24.cloned.1.call-update) | async-done | bytes 1228816 | tf_op jit(solution)/shard_map/reduce_scatter | solution.py:280
  444.5 47.8 %reduce-scatter.26.cloned.1.call-done = bf16[240,2560]{1,0:T(8,128)(2,1)} async-done(((bf16[960,2560]{1,0:T(8,128)(2,1)}), bf16[240,2560]{1,0:T(8,128)(2,1)}) %reduce-scatter.26.cloned.1.call-update) | async-done | bytes 1228816 | tf_op jit(solution)/shard_map/reduce_scatter | solution.py:283
  496.3 49.8 %reduce-scatter.38.cloned.1.call-done = bf16[640,960]{1,0:T(8,128)(2,1)} async-done(((bf16[2560,960]{1,0:T(8,128)(2,1)}), bf16[640,960]{1,0:T(8,128)(2,1)}) %reduce-scatter.38.cloned.1.call-update) | async-done | bytes 1228816 | tf_op jit(solution)/shard_map/reduce_scatter | solution.py:286
  552.1 173.2 %all-reduce.10.cloned.1.call-done = bf16[2457600]{0:T(1024)(128)(2,1)} async-done(((bf16[2457600]{0:T(1024)(128)(2,1)}), bf16[2457600]{0:T(1024)(128)(2,1)}) %all-reduce.10.cloned.1.call-update) | async-done | bytes 4915216
  735.1 6.7 all-reduce.6
  741.9 21.1 %all-reduce.5 = (f32[240]{0:T(256)}, f32[240]{0:T(256)}) all-reduce(f32[240]{0:T(256)S(1)} %get-tuple-element.264, f32[240]{0:T(256)S(1)} %get-tuple-element.263), channel_id=1, replica_groups=mesh['rep'=8,'shard'=4] {'rep'}, use_global_device_ids=true, to_apply=%region_15.16 | all-reduce | flops 480 | bytes 3840 | tf_op jit(solution)/shard_map/psum | solution.py:298
  764.0 45.1 %all-gather.19.cloned.1.call-done = bf16[2457600]{0:T(1024)(128)(2,1)} async-done(((bf16[307200]{0:T(1024)(128)(2,1)}), bf16[2457600]{0:T(1024)(128)(2,1)}) %all-gather.19.cloned.1.call-update) | async-done | bytes 4915216 | tf_op jit(solution)/shard_map/all_gather | solution.py:295
  809.1 5.2 fusion.97
  (287 shorter events, 146.6 us)
Async XLA Ops:
  7.2 53.0 %all-gather.9.cloned.1.call-start = ((), (), s32[]{:S(2)}) async-start(), calls=%async_computation.9 | async-start | bytes 2457600 | tf_op jit(solution)/shard_map/all_gather | solution.py:112
  7.9 60.3 %all-gather.11.cloned.1.call-start = ((), (), s32[]{:S(2)}) async-start(), calls=%async_computation.10 | async-start | bytes 2457600 | tf_op jit(solution)/shard_map/all_gather | solution.py:115
  10.0 93.7 %all-gather.13.cloned.1.call-start = ((), (), s32[]{:S(2)}) async-start(), calls=%async_computation.11 | async-start | bytes 6144000 | tf_op jit(solution)/shard_map/all_gather | solution.py:117
  10.8 132.9 %all-gather.15.cloned.1.call-start = ((), (), s32[]{:S(2)}) async-start(), calls=%async_computation.12 | async-start | bytes 6144000 | tf_op jit(solution)/shard_map/all_gather | solution.py:118
  11.3 172.3 %all-gather.17.cloned.1.call-start = ((), (), s32[]{:S(2)}) async-start(), calls=%async_computation.13 | async-start | bytes 6144000 | tf_op jit(solution)/shard_map/all_gather | solution.py:119
  11.9 233.9 %reduce-scatter.28.cloned.1.call-start = ((), (), s32[]{:S(2)}) async-start(), calls=%async_computation.18 | async-start | bytes 491520
  22.3 40.7 %copy-start.23 = (f32[960]{0:T(1024)}, f32[960]{0:T(1024)S(1)}, u32[]{:S(2)}) copy-start(f32[960]{0:T(1024)S(1)} %convert_element_type.193) | copy-start | bytes 11524
  22.5 40.6 %copy-start.28 = (f32[128]{0:T(128)}, f32[128]{0:T(128)S(1)}, u32[]{:S(2)}) copy-start(f32[128]{0:T(128)S(1)} %add_rsqrt_fusion.1) | copy-start | bytes 1540
  35.1 15.9 %copy-start.5 = (bf16[960,320]{0,1:T(8,128)(2,1)}, bf16[960,320]{0,1:T(8,128)(2,1)S(1)}, u32[]{:S(2)}) copy-start(bf16[960,320]{0,1:T(8,128)(2,1)S(1)} %reshape.438) | copy-start | bytes 1843204
  68.2 39.8 %copy-start.19 = (bf16[5,512,64]{1,2,0:T(8,128)(2,1)}, bf16[5,512,64]{1,2,0:T(8,128)(2,1)S(1)}, u32[]{:S(2)}) copy-start(bf16[5,512,64]{1,2,0:T(8,128)(2,1)S(1)} %get-tuple-element.523) | copy-start | bytes 983044
  108.0 75.6 %copy-start.16 = (bf16[1,128,960]{1,2,0:T(8,128)(2,1)S(1)}, bf16[1,128,960]{1,2,0:T(8,128)(2,1)}, u32[]{:S(2)}) copy-start(bf16[1,128,960]{1,2,0:T(8,128)(2,1)} %param.16) | copy-start | bytes 737284
  222.9 25.7 %copy-start.7 = (bf16[5,128,3,64]{1,3,2,0:T(8,128)(2,1)}, bf16[5,128,3,64]{1,3,2,0:T(8,128)(2,1)S(1)}, u32[]{:S(2)}) copy-start(bf16[5,128,3,64]{1,3,2,0:T(8,128)(2,1)S(1)} %get-tuple-element.509) | copy-start | bytes 737284
  222.9 24.0 %copy-start.24 = (f32[960]{0:T(1024)S(1)}, f32[960]{0:T(1024)}, u32[]{:S(2)}) copy-start(f32[960]{0:T(1024)} %copy-done.23) | copy-start | bytes 11524
  222.9 24.0 %copy-start.29 = (f32[128]{0:T(128)S(1)}, f32[128]{0:T(128)}, u32[]{:S(2)}) copy-start(f32[128]{0:T(128)} %copy-done.28) | copy-start | bytes 1540
  224.9 44.8 %reduce-scatter.30.cloned.1.call-start = ((), (), s32[]{:S(2)}) async-start(), calls=%async_computation.19 | async-start | bytes 491520
  226.9 74.3 %reduce-scatter.32.cloned.1.call-start = ((), (), s32[]{:S(2)}) async-start(), calls=%async_computation.20 | async-start | bytes 921600 | tf_op jit(solution)/shard_map/reduce_scatter | solution.py:268
  248.6 73.3 %reduce-scatter.34.cloned.1.call-start = ((), (), s32[]{:S(2)}) async-start(), calls=%async_computation.21 | async-start | bytes 921600 | tf_op jit(solution)/shard_map/reduce_scatter | solution.py:271
  272.3 83.0 %reduce-scatter.22.cloned.1.call-start = ((), (), s32[]{:S(2)}) async-start(), calls=%async_computation.14 | async-start | bytes 2457600 | tf_op jit(solution)/shard_map/reduce_scatter | solution.py:265
  274.5 114.3 %reduce-scatter.36.cloned.1.call-start = ((), (), s32[]{:S(2)}) async-start(), calls=%async_computation.22 | async-start | bytes 2457600
  278.8 161.7 %reduce-scatter.24.cloned.1.call-start = ((), (), s32[]{:S(2)}) async-start(), calls=%async_computation.15 | async-start | bytes 6144000 | tf_op jit(solution)/shard_map/reduce_scatter | solution.py:280
  283.7 208.7 %reduce-scatter.26.cloned.1.call-start = ((), (), s32[]{:S(2)}) async-start(), calls=%async_computation.16 | async-start | bytes 6144000 | tf_op jit(solution)/shard_map/reduce_scatter | solution.py:283
  288.4 257.7 %reduce-scatter.38.cloned.1.call-start = ((), (), s32[]{:S(2)}) async-start(), calls=%async_computation.23 | async-start | bytes 6553600 | tf_op jit(solution)/shard_map/reduce_scatter | solution.py:286
  301.0 424.2 %all-reduce.10.cloned.1.call-start = ((), (), s32[]{:S(2)}) async-start(), calls=%async_computation.24 | async-start | bytes 9830400
  550.3 258.8 %all-gather.19.cloned.1.call-start = ((), (), s32[]{:S(2)}) async-start(), calls=%async_computation.17 | async-start | bytes 5529600 | tf_op jit(solution)/shard_map/all_gather | solution.py:295
  (28 other events, 104.0 us)
Sparse Core Ops, SparseCore 0:
  9.5 28.1 all-gather.8
  39.8 23.5 all-gather.10
  65.0 38.6 all-gather.12
  105.1 38.5 all-gather.14
  145.1 38.4 all-gather.16
  225.0 20.7 reduce-scatter.27
  248.9 20.7 reduce-scatter.29
  272.8 22.9 reduce-scatter.31
  298.9 22.9 reduce-scatter.33
  324.9 30.3 reduce-scatter.21
  358.4 30.3 reduce-scatter.35
  391.3 49.2 reduce-scatter.23
  443.1 49.2 reduce-scatter.25
  494.7 51.3 reduce-scatter.37
  550.4 174.8 all-reduce.9
  727.9 81.1 all-gather.18
where the time goes:
time: 840 us; the launch traced here: 838 us
  waiting for transfers between devices  592 us (70%)
  matrix products  77.6 us (9%)
  local copies, waits for them, and re-layouts  75.7 us (9%)
  blocking collectives  70.6 us (8%)
  between operations  16.6 us (2%)
    unnamed x20, waiting for transfers between devices  247 us
    reduce_scatter x1, waiting for transfers between devices, local(): lax.psum_scatter(grad_down.astype(jnp.bfloat16), 'shard', scatter_dimensi...  49.8 us
    reduce_scatter x1, waiting for transfers between devices, local(): lax.psum_scatter(grad_wup.astype(jnp.bfloat16), 'shard', scatter_dimensio...  47.8 us
    reduce_scatter x1, waiting for transfers between devices, local(): lax.psum_scatter(grad_wgate.astype(jnp.bfloat16), 'shard', scatter_dimens...  47.2 us
    all_gather x1, waiting for transfers between devices, local(): lax.all_gather(share.astype(jnp.bfloat16), 'rep', axis=0, tiled=True)  45.1 us
    unnamed x99, local copies, waits for them, and re-layouts  38.3 us
    all_gather x1, waiting for transfers between devices, local(): lax.all_gather(up_weight, 'shard', axis=0, tiled=True)  35.7 us
    all_gather x1, waiting for transfers between devices, local(): lax.all_gather(down_weight, 'shard', axis=0, tiled=True)  35.6 us
  transfers between devices with their start and end apart: 16, of which 13 were waited for; matrix products, arithmetic and copies ran while one was open for 10% of the time, Pallas kernels for 0%

commit v1 on v0

--- a/solution.py
+++ b/solution.py
@@ -14,6 +14,24 @@
 SCALE = 0.125
 NEGATIVE = -1e30
 THETA = 10000.0
+
+
+def gather_around(shard, axis, dim):
+    ways, here, turn = (lax.axis_size(axis), lax.axis_index(axis), shard.shape[dim])
+    lengths = [n * ways if d == dim else n for d, n in enumerate(shard.shape)]
+    full = lax.dynamic_update_slice_in_dim(
+        jnp.zeros(lengths, shard.dtype), shard, here * turn, axis=dim
+    )
+    going_up = going_down = shard
+    for far in range(1, ways // 2 + 1):
+        going_up = lax.ppermute(going_up, axis, [(d, (d + 1) % ways) for d in range(ways)])
+        full = lax.dynamic_update_slice_in_dim(full, going_up, (here - far) % ways * turn, axis=dim)
+        if 2 * far < ways:
+            going_down = lax.ppermute(going_down, axis, [(d, (d - 1) % ways) for d in range(ways)])
+            full = lax.dynamic_update_slice_in_dim(
+                full, going_down, (here + far) % ways * turn, axis=dim
+            )
+    return full
 
 
 def rms_inverse(rows):
@@ -292,9 +310,7 @@
     share = lax.psum_scatter(
         flat_all.astype(jnp.bfloat16), "rep", scatter_dimension=0, tiled=True
     ).astype(jnp.float32)
-    whole = lax.all_gather(share.astype(jnp.bfloat16), "rep", axis=0, tiled=True).astype(
-        share.dtype
-    )
+    whole = gather_around(share.astype(jnp.bfloat16), "rep", 0).astype(share.dtype)
     gains_sum = lax.psum((owned[0], owned[5]), "rep")
     pieces_back = []
     offset = 0

time: 840 us -> 975 us (1.16); the launches traced: 838 us -> 961 us
  local copies, waits for them, and re-layouts: 75.7 us -> 156 us
  waiting for transfers between devices: 592 us -> 609 us
  starting transfers between devices: 1.13 us -> 17.8 us
    dynamic_update_slice x0 -> x8, local copies, waits for them, and re-layouts: none -> 74.6 us  [the longest x4 41.4 us: gather_around(): lax.dynamic_update_slice_in_dim(full, going_up, (here - far) % ways * tur...]
    ppermute x0 -> x7, waiting for transfers between devices: none -> 63 us  [the longest x4 63 us: gather_around(): lax.ppermute(going_up, axis, [(d, (d + 1) % ways) for d in range(ways)])]
    all_gather x1 -> x0, waiting for transfers between devices: 45.1 us -> none  [local(): lax.all_gather(share.astype(jnp.bfloat16), 'rep', axis=0, tiled=True)]
    ppermute x0 -> x7, starting transfers between devices: none -> 17 us  [the longest x4 9.12 us: gather_around(): lax.ppermute(going_up, axis, [(d, (d + 1) % ways) for d in range(ways)])]
    unnamed x99 -> x100, local copies, waits for them, and re-layouts: 38.3 us -> 33.3 us
    unnamed x20 -> x19, waiting for transfers between devices: 247 us -> 248 us
  transfers between devices with their start and end apart: 16 -> 22, of which waited for: 13 -> 15; matrix products, arithmetic and copies ran while one was open for 10% -> 16% of each run, Pallas kernels for 0% -> 0%
where the time goes in v1:
time: 975 us; the launch traced here: 961 us
  waiting for transfers between devices  609 us (62%)
  local copies, waits for them, and re-layouts  156 us (16%)
  matrix products  85.5 us (9%)
  blocking collectives  69 us (7%)
  starting transfers between devices  17.8 us (2%)
  between operations  16.9 us (2%)
    unnamed x19, waiting for transfers between devices  248 us
    ppermute x4, waiting for transfers between devices, gather_around(): lax.ppermute(going_up, axis, [(d, (d + 1) % ways) for d in range(ways)])  63 us
    reduce_scatter x1, waiting for transfers between devices, local(): lax.psum_scatter(grad_down.astype(jnp.bfloat16), 'shard', scatter_dimensi...  49.8 us
    reduce_scatter x1, waiting for transfers between devices, local(): lax.psum_scatter(grad_wup.astype(jnp.bfloat16), 'shard', scatter_dimensio...  47.8 us
    reduce_scatter x1, waiting for transfers between devices, local(): lax.psum_scatter(grad_wgate.astype(jnp.bfloat16), 'shard', scatter_dimens...  47.2 us
    dynamic_update_slice x4, local copies, waits for them, and re-layouts, gather_around(): lax.dynamic_update_slice_in_dim(full, going_up, (here - far) % ways * tur...  41.4 us
    all_gather x1, waiting for transfers between devices, local(): lax.all_gather(up_weight, 'shard', axis=0, tiled=True)  35.7 us
    all_gather x1, waiting for transfers between devices, local(): lax.all_gather(down_weight, 'shard', axis=0, tiled=True)  35.6 us
  transfers between devices with their start and end apart: 22, of which 15 were waited for; matrix products, arithmetic and copies ran while one was open for 16% of the time, Pallas kernels for 0%

profile of v1, /device:TPU:0, one launch (start us, length us, event | category | flops | bytes accessed | tf_op | source)
XLA Modules:
  0.0 961.2 jit_solution(4228612902017331762)
XLA Ops:
  22.5 11.5 %all-gather.1 = bf16[4,240,320]{1,2,0:T(8,128)(2,1)S(1)} all-gather(bf16[1,240,320]{1,2,0:T(8,128)(2,1)S(1)} %bitcast.327), channel_id=1, replica_groups=mesh['rep'=8,'shard'=4] {'shard'}, dimensions={0}, use_global_device_ids=true | all-gather | bytes 768000 | tf_op jit(solution)/shard_map/all_gather | solution.py:131
  74.7 29.0 %all-gather.12.cloned.1.call-done = bf16[960,2560]{1,0:T(8,128)(2,1)} async-done(((bf16[240,2560]{1,0:T(8,128)(2,1)}), bf16[960,2560]{1,0:T(8,128)(2,1)}) %all-gather.12.cloned.1.call-update) | async-done | bytes 4915216 | tf_op jit(solution)/shard_map/all_gather | solution.py:135
  108.0 35.7 %all-gather.14.cloned.1.call-done = bf16[960,2560]{1,0:T(8,128)(2,1)} async-done(((bf16[240,2560]{1,0:T(8,128)(2,1)}), bf16[960,2560]{1,0:T(8,128)(2,1)}) %all-gather.14.cloned.1.call-update) | async-done | bytes 4915216 | tf_op jit(solution)/shard_map/all_gather | solution.py:136
  148.1 35.6 %all-gather.16.cloned.1.call-done = bf16[2560,960]{0,1:T(8,128)(2,1)} async-done(((bf16[640,960]{0,1:T(8,128)(2,1)}), bf16[2560,960]{0,1:T(8,128)(2,1)}) %all-gather.16.cloned.1.call-update) | async-done | bytes 4915216 | tf_op jit(solution)/shard_map/all_gather | solution.py:137
  196.8 36.9 %while.31 = (s32[]{:T(128)}, f32[5,128,3,64]{1,3,2,0:T(8,128)}, bf16[5,512,64]{1,2,0:T(8,128)(2,1)}, bf16[5,512,64]{1,2,0:T(8,128)(2,1)}, bf16[5,512,64]{1,2,0:T...) while((s32[]{:T(128)}, f32[5,128,3,64]{1,3,2,0:T(8,128)}, ...), condition=%wide.region_9.10_spmd.clone.clone, body=%wide.region_7.9_spmd.clone.sunk.clone | while | flops 127762176 | bytes 4536441 | solution.py:229
  237.7 19.0 %reduce-scatter.28.cloned.1.call-done = bf16[128,320]{1,0:T(8,128)(2,1)} async-done(((bf16[512,320]{1,0:T(8,128)(2,1)}), bf16[128,320]{1,0:T(8,128)(2,1)}) %reduce-scatter.28.cloned.1.call-update) | async-done | bytes 81936
  259.4 21.1 %reduce-scatter.30.cloned.1.call-done = bf16[128,320]{1,0:T(8,128)(2,1)} async-done(((bf16[512,320]{1,0:T(8,128)(2,1)}), bf16[128,320]{1,0:T(8,128)(2,1)}) %reduce-scatter.30.cloned.1.call-update) | async-done | bytes 81936
  311.2 21.5 %reduce-scatter.34.cloned.1.call-done = bf16[240,320]{1,0:T(8,128)(2,1)} async-done(((bf16[960,320]{1,0:T(8,128)(2,1)}), bf16[240,320]{1,0:T(8,128)(2,1)}) %reduce-scatter.34.cloned.1.call-update) | async-done | bytes 153616 | tf_op jit(solution)/shard_map/reduce_scatter | solution.py:289
  333.9 32.2 %reduce-scatter.22.cloned.1.call-done = bf16[240,960]{1,0:T(8,128)(2,1)} async-done(((bf16[960,960]{1,0:T(8,128)(2,1)}), bf16[240,960]{1,0:T(8,128)(2,1)}) %reduce-scatter.22.cloned.1.call-update) | async-done | bytes 460816 | tf_op jit(solution)/shard_map/reduce_scatter | solution.py:283
  368.5 31.1 %reduce-scatter.36.cloned.1.call-done = bf16[240,960]{1,0:T(8,128)(2,1)} async-done(((bf16[960,960]{1,0:T(8,128)(2,1)}), bf16[240,960]{1,0:T(8,128)(2,1)}) %reduce-scatter.36.cloned.1.call-update) | async-done | bytes 460816
  404.1 47.2 %reduce-scatter.24.cloned.1.call-done = bf16[240,2560]{1,0:T(8,128)(2,1)} async-done(((bf16[960,2560]{1,0:T(8,128)(2,1)}), bf16[240,2560]{1,0:T(8,128)(2,1)}) %reduce-scatter.24.cloned.1.call-update) | async-done | bytes 1228816 | tf_op jit(solution)/shard_map/reduce_scatter | solution.py:298
  455.3 47.8 %reduce-scatter.26.cloned.1.call-done = bf16[240,2560]{1,0:T(8,128)(2,1)} async-done(((bf16[960,2560]{1,0:T(8,128)(2,1)}), bf16[240,2560]{1,0:T(8,128)(2,1)}) %reduce-scatter.26.cloned.1.call-update) | async-done | bytes 1228816 | tf_op jit(solution)/shard_map/reduce_scatter | solution.py:301
  507.1 49.8 %reduce-scatter.38.cloned.1.call-done = bf16[640,960]{1,0:T(8,128)(2,1)} async-done(((bf16[2560,960]{1,0:T(8,128)(2,1)}), bf16[640,960]{1,0:T(8,128)(2,1)}) %reduce-scatter.38.cloned.1.call-update) | async-done | bytes 1228816 | tf_op jit(solution)/shard_map/reduce_scatter | solution.py:304
  562.3 173.7 %all-reduce.10.cloned.1.call-done = bf16[2457600]{0:T(1024)(128)(2,1)} async-done(((bf16[2457600]{0:T(1024)(128)(2,1)}), bf16[2457600]{0:T(1024)(128)(2,1)}) %all-reduce.10.cloned.1.call-update) | async-done | bytes 4915216
  745.6 23.1 %collective-permute-done = bf16[307200]{0:T(1024)(128)(2,1)} collective-permute-done((bf16[307200]{0:T(1024)(128)(2,1)}, bf16[307200]{0:T(1024)(128)(2,1)}, u32[]{:S(2)}, u32[]{:S(2)}) %collective-permute-start) | collective-permute-done | bytes 614432 | tf_op jit(solution)/shard_map/ppermute | solution.py:27
  774.2 22.8 %collective-permute-done.2 = bf16[307200]{0:T(1024)(128)(2,1)} collective-permute-done((bf16[307200]{0:T(1024)(128)(2,1)}, bf16[307200]{0:T(1024)(128)(2,1)}, u32[]{:S(2)}, u32[]{:S(2)}) %collective-permute-start.2) | collective-permute-done | bytes 614432 | tf_op jit(solution)/shard_map/ppermute | solution.py:27
  807.7 17.1 %collective-permute-done.4 = bf16[307200]{0:T(1024)(128)(2,1)} collective-permute-done((bf16[307200]{0:T(1024)(128)(2,1)}, bf16[307200]{0:T(1024)(128)(2,1)}, u32[]{:S(2)}, u32[]{:S(2)}) %collective-permute-start.4) | collective-permute-done | bytes 614432 | tf_op jit(solution)/shard_map/ppermute | solution.py:27
  834.2 19.9 %all-reduce.5 = (f32[240]{0:T(256)}, f32[240]{0:T(256)}) all-reduce(f32[240]{0:T(256)S(1)} %get-tuple-element.266, f32[240]{0:T(256)S(1)} %get-tuple-element.265), channel_id=1, replica_groups=mesh['rep'=8,'shard'=4] {'rep'}, use_global_device_ids=true, to_apply=%region_15.16 | all-reduce | flops 480 | bytes 3840 | tf_op jit(solution)/shard_map/psum | solution.py:314
  855.1 10.4 %dynamic_update_slice.43 = bf16[2457600]{0:T(1024)(128)(2,1)} dynamic-update-slice(bf16[2457600]{0:T(1024)(128)(2,1)} %get-tuple-element.235, bf16[307200]{0:T(1024)(128)(2,1)} %collective-permute-done, s32[]{:T(128)S(6)} %select_n.89) | dynamic-update-slice | bytes 1228804 | tf_op jit(solution)/shard_map/dynamic_update_slice | solution.py:28
  865.5 10.4 %dynamic_update_slice.44 = bf16[2457600]{0:T(1024)(128)(2,1)} dynamic-update-slice(bf16[2457600]{0:T(1024)(128)(2,1)} %dynamic_update_slice.43, bf16[307200]{0:T(1024)(128)(2,1)} %collective-permute-done.1, s32[]{:T(128)S(6)} %select_n.91) | dynamic-update-slice | bytes 1228804 | tf_op jit(solution)/shard_map/dynamic_update_slice | solution.py:31
  886.2 10.3 %dynamic_update_slice.46 = bf16[2457600]{0:T(1024)(128)(2,1)} dynamic-update-slice(bf16[2457600]{0:T(1024)(128)(2,1)} %dynamic_update_slice.45, bf16[307200]{0:T(1024)(128)(2,1)} %collective-permute-done.3, s32[]{:T(128)S(6)} %select_n.95) | dynamic-update-slice | bytes 1228804 | tf_op jit(solution)/shard_map/dynamic_update_slice | solution.py:31
  896.5 10.4 %dynamic_update_slice.47 = bf16[2457600]{0:T(1024)(128)(2,1)} dynamic-update-slice(bf16[2457600]{0:T(1024)(128)(2,1)} %dynamic_update_slice.46, bf16[307200]{0:T(1024)(128)(2,1)} %collective-permute-done.4, s32[]{:T(128)S(6)} %select_n.97) | dynamic-update-slice | bytes 1228804 | tf_op jit(solution)/shard_map/dynamic_update_slice | solution.py:28
  906.9 10.3 %dynamic_update_slice.48 = bf16[2457600]{0:T(1024)(128)(2,1)} dynamic-update-slice(bf16[2457600]{0:T(1024)(128)(2,1)} %dynamic_update_slice.47, bf16[307200]{0:T(1024)(128)(2,1)} %collective-permute-done.5, s32[]{:T(128)S(6)} %select_n.99) | dynamic-update-slice | bytes 1228804 | tf_op jit(solution)/shard_map/dynamic_update_slice | solution.py:31
  917.2 10.4 %dynamic_update_slice.49 = bf16[2457600]{0:T(1024)(128)(2,1)} dynamic-update-slice(bf16[2457600]{0:T(1024)(128)(2,1)} %dynamic_update_slice.48, bf16[307200]{0:T(1024)(128)(2,1)} %collective-permute-done.6, s32[]{:T(128)S(6)} %select_n.101) | dynamic-update-slice | bytes 1228804 | tf_op jit(solution)/shard_map/dynamic_update_slice | solution.py:28
  (308 shorter events, 250.7 us)
Async XLA Ops:
  7.2 53.2 %all-gather.8.cloned.1.call-start = ((), (), s32[]{:S(2)}) async-start(), calls=%async_computation.9 | async-start | bytes 2457600 | tf_op jit(solution)/shard_map/all_gather | solution.py:130
  8.0 63.4 %all-gather.10.cloned.1.call-start = ((), (), s32[]{:S(2)}) async-start(), calls=%async_computation.10 | async-start | bytes 2457600 | tf_op jit(solution)/shard_map/all_gather | solution.py:133
  10.1 93.6 %all-gather.12.cloned.1.call-start = ((), (), s32[]{:S(2)}) async-start(), calls=%async_computation.11 | async-start | bytes 6144000 | tf_op jit(solution)/shard_map/all_gather | solution.py:135
  10.8 132.9 %all-gather.14.cloned.1.call-start = ((), (), s32[]{:S(2)}) async-start(), calls=%async_computation.12 | async-start | bytes 6144000 | tf_op jit(solution)/shard_map/all_gather | solution.py:136
  11.4 172.3 %all-gather.16.cloned.1.call-start = ((), (), s32[]{:S(2)}) async-start(), calls=%async_computation.13 | async-start | bytes 6144000 | tf_op jit(solution)/shard_map/all_gather | solution.py:137
  12.0 244.7 %reduce-scatter.28.cloned.1.call-start = ((), (), s32[]{:S(2)}) async-start(), calls=%async_computation.17 | async-start | bytes 491520
  74.7 109.0 %copy-start.17 = (bf16[1,128,960]{1,2,0:T(8,128)(2,1)S(1)}, bf16[1,128,960]{1,2,0:T(8,128)(2,1)}, u32[]{:S(2)}) copy-start(bf16[1,128,960]{1,2,0:T(8,128)(2,1)} %param.16) | copy-start | bytes 737284
  235.7 44.9 %reduce-scatter.30.cloned.1.call-start = ((), (), s32[]{:S(2)}) async-start(), calls=%async_computation.18 | async-start | bytes 491520
  237.6 72.4 %reduce-scatter.32.cloned.1.call-start = ((), (), s32[]{:S(2)}) async-start(), calls=%async_computation.19 | async-start | bytes 921600 | tf_op jit(solution)/shard_map/reduce_scatter | solution.py:286
  259.4 73.3 %reduce-scatter.34.cloned.1.call-start = ((), (), s32[]{:S(2)}) async-start(), calls=%async_computation.20 | async-start | bytes 921600 | tf_op jit(solution)/shard_map/reduce_scatter | solution.py:289
  283.1 83.0 %reduce-scatter.22.cloned.1.call-start = ((), (), s32[]{:S(2)}) async-start(), calls=%async_computation.14 | async-start | bytes 2457600 | tf_op jit(solution)/shard_map/reduce_scatter | solution.py:283
  285.3 114.3 %reduce-scatter.36.cloned.1.call-start = ((), (), s32[]{:S(2)}) async-start(), calls=%async_computation.21 | async-start | bytes 2457600
  289.6 161.7 %reduce-scatter.24.cloned.1.call-start = ((), (), s32[]{:S(2)}) async-start(), calls=%async_computation.15 | async-start | bytes 6144000 | tf_op jit(solution)/shard_map/reduce_scatter | solution.py:298
  294.6 208.6 %reduce-scatter.26.cloned.1.call-start = ((), (), s32[]{:S(2)}) async-start(), calls=%async_computation.16 | async-start | bytes 6144000 | tf_op jit(solution)/shard_map/reduce_scatter | solution.py:301
  298.2 258.6 %reduce-scatter.38.cloned.1.call-start = ((), (), s32[]{:S(2)}) async-start(), calls=%async_computation.22 | async-start | bytes 6553600 | tf_op jit(solution)/shard_map/reduce_scatter | solution.py:304
  309.9 426.1 %all-reduce.10.cloned.1.call-start = ((), (), s32[]{:S(2)}) async-start(), calls=%async_computation.23 | async-start | bytes 9830400
  740.8 86.5 %copy-start.31 = (f32[128]{0:T(128)S(1)}, f32[128]{0:T(128)}, u32[]{:S(2)}) copy-start(f32[128]{0:T(128)} %copy-done.29) | copy-start | bytes 1540
  740.8 27.9 %collective-permute-start = (bf16[307200]{0:T(1024)(128)(2,1)}, bf16[307200]{0:T(1024)(128)(2,1)}, u32[]{:S(2)}, u32[]{:S(2)}) collective-permute-start(bf16[307200]{0:T(1024)(128)(2,1)} %get-tuple-element.236), channel_id=1, source_target_pairs={{0,4},{4,8},{8,12},{12,16},{16,20},{20,24},{24,28},{28,0},{1,5},{5... | collective-permute-start | bytes 1843208 | tf_op jit(solution)/shard_map/ppermute | solution.py:27
  742.3 29.6 %collective-permute-start.1 = (bf16[307200]{0:T(1024)(128)(2,1)}, bf16[307200]{0:T(1024)(128)(2,1)}, u32[]{:S(2)}, u32[]{:S(2)}) collective-permute-start(bf16[307200]{0:T(1024)(128)(2,1)} %get-tuple-element.236), channel_id=1, source_target_pairs={{0,28},{4,0},{8,4},{12,8},{16,12},{20,16},{24,20},{28,24},{1,29},{... | collective-permute-start | bytes 1843208 | tf_op jit(solution)/shard_map/ppermute | solution.py:30
  768.7 28.3 %collective-permute-start.2 = (bf16[307200]{0:T(1024)(128)(2,1)}, bf16[307200]{0:T(1024)(128)(2,1)}, u32[]{:S(2)}, u32[]{:S(2)}) collective-permute-start(bf16[307200]{0:T(1024)(128)(2,1)} %collective-permute-done), channel_id=1, source_target_pairs={{0,4},{4,8},{8,12},{12,16},{16,20},{20,24},{24,28},{28,0},{1,5},{5... | collective-permute-start | bytes 1843208 | tf_op jit(solution)/shard_map/ppermute | solution.py:27
  771.9 33.5 %collective-permute-start.3 = (bf16[307200]{0:T(1024)(128)(2,1)}, bf16[307200]{0:T(1024)(128)(2,1)}, u32[]{:S(2)}, u32[]{:S(2)}) collective-permute-start(bf16[307200]{0:T(1024)(128)(2,1)} %collective-permute-done.1), channel_id=1, source_target_pairs={{0,28},{4,0},{8,4},{12,8},{16,12},{20,16},{24,20},{28,24},{1,29},{... | collective-permute-start | bytes 1843208 | tf_op jit(solution)/shard_map/ppermute | solution.py:30
  797.0 27.8 %collective-permute-start.4 = (bf16[307200]{0:T(1024)(128)(2,1)}, bf16[307200]{0:T(1024)(128)(2,1)}, u32[]{:S(2)}, u32[]{:S(2)}) collective-permute-start(bf16[307200]{0:T(1024)(128)(2,1)} %collective-permute-done.2), channel_id=1, source_target_pairs={{0,4},{4,8},{8,12},{12,16},{16,20},{20,24},{24,28},{28,0},{1,5},{5... | collective-permute-start | bytes 1843208 | tf_op jit(solution)/shard_map/ppermute | solution.py:27
  805.4 101.4 %collective-permute-start.5 = (bf16[307200]{0:T(1024)(128)(2,1)}, bf16[307200]{0:T(1024)(128)(2,1)}, u32[]{:S(2)}, u32[]{:S(2)}) collective-permute-start(bf16[307200]{0:T(1024)(128)(2,1)} %collective-permute-done.3), channel_id=1, source_target_pairs={{0,28},{4,0},{8,4},{12,8},{16,12},{20,16},{24,20},{28,24},{1,29},{... | collective-permute-start | bytes 1843208 | tf_op jit(solution)/shard_map/ppermute | solution.py:30
  824.8 92.4 %collective-permute-start.6 = (bf16[307200]{0:T(1024)(128)(2,1)}, bf16[307200]{0:T(1024)(128)(2,1)}, u32[]{:S(2)}, u32[]{:S(2)}) collective-permute-start(bf16[307200]{0:T(1024)(128)(2,1)} %collective-permute-done.4), channel_id=1, source_target_pairs={{0,4},{4,8},{8,12},{12,16},{16,20},{20,24},{24,28},{28,0},{1,5},{5... | collective-permute-start | bytes 1843208 | tf_op jit(solution)/shard_map/ppermute | solution.py:27
  (35 other events, 971.5 us)
Sparse Core Ops, SparseCore 0:
  9.6 28.1 all-gather.7
  39.9 23.5 all-gather.9
  65.1 38.5 all-gather.11
  105.1 38.5 all-gather.13
  145.1 38.4 all-gather.15
  235.8 20.8 reduce-scatter.27
  259.7 20.8 reduce-scatter.29
  283.7 22.9 reduce-scatter.31
  309.7 22.9 reduce-scatter.33
  335.7 30.3 reduce-scatter.21
  369.2 30.3 reduce-scatter.35
  402.1 49.2 reduce-scatter.23
  453.9 49.1 reduce-scatter.25
  505.5 51.3 reduce-scatter.37
  561.2 174.8 all-reduce.9
